TPU v7x, 32 devices: a whole 2x2x4 slice. The times are simulated.
32 devices in a mesh: gx: 4 (over z), gy: 8 (over y, x, core).
Axes of the slice: x: 2, y: 2, z: 4, core: 2. Of those that a mesh axis runs over, the one named last changes fastest.
Arguments:
- source: float32 [64, 256, 512], P('gx', 'gy')
- voxel_phase: int32 [64, 256, 512], P('gx', 'gy'), may hold values from 0 to 2
- lin_potential: float32 [64, 256, 512], P('gx', 'gy'), may hold values from -1 to 1
- link_voxel: int32 [4, 8, 2048], P('gx', 'gy'), may hold values from 0 to 262143
- link_count: int32 [4, 8, 8], P('gx', 'gy'), may hold values from 1 to 256, as said below
- link_target: int32 [4, 8, 2048], P('gx', 'gy'), may hold values from 0 to 511
Outputs:
- solution: float32 [64, 256, 512], P('gx', 'gy')
- particle_current: float32 [4, 8, 512], P('gx', 'gy')
Inputs may be any that keep to these rules, and one draw needn't show every extreme that they name: `link_count`: every device has exactly 256 live links to at least one gy peer.
All inputs are finite; a program needn't handle non-finite values.
Results may differ from a plain program's by a relative error of at most 0.00012.
Values sent between devices are 32-bit elements; how exact they have to be, the bound alone decides.
A program may use at most 128 MiB of HBM per device.

v0:
```python
import jax
import jax.numpy as jnp
from jax import lax
from jax.sharding import PartitionSpec as P

ITERS = 12
PART_DEV = 512


def extended(block, sides, width):
    for axis, dim in sides:
        count = lax.axis_size(axis)
        forward = [(i, i + 1) for i in range(count - 1)]
        backward = [(target, source) for source, target in forward]
        low = lax.ppermute(
            lax.slice_in_dim(block, block.shape[dim] - width, None, axis=dim), axis, forward
        )
        high = lax.ppermute(lax.slice_in_dim(block, 0, width, axis=dim), axis, backward)
        block = jnp.concatenate([low, block, high], axis=dim)
    return block


def rate_of(voxel_phase):
    return jnp.where(voxel_phase == 1, 0.3, jnp.where(voxel_phase == 2, 0.08, 0.02)).astype(
        jnp.float32
    )


def butler(lin_potential):
    rising = jnp.exp(0.4 * lin_potential)
    falling = jnp.exp(-0.6 * lin_potential)
    return (rising - falling, 0.4 * rising + 0.6 * falling)


def operate(values, diagonal):
    padded = extended(values, (("gx", 0), ("gy", 1)), 1)
    padded = jnp.pad(padded, ((0, 0), (0, 0), (1, 1)))
    beside = padded[2:, 1:-1, 1:-1] + padded[:-2, 1:-1, 1:-1]
    beside = beside + padded[1:-1, 2:, 1:-1] + padded[1:-1, :-2, 1:-1]
    beside = beside + padded[1:-1, 1:-1, 2:] + padded[1:-1, 1:-1, :-2]
    return diagonal * values - beside


def paired_sums(residual, precond, image):
    return lax.psum((jnp.sum(residual * precond), jnp.sum(precond * image)), ("gx", "gy"))


def shards(source, voxel_phase, lin_potential, link_voxel, link_count, link_target):
    base, slope = butler(lin_potential)
    diagonal = 6.0 + rate_of(voxel_phase) * slope
    solution = jnp.zeros_like(source)
    residual = source
    precond = residual / diagonal
    image = operate(precond, diagonal)
    norm_now, product = paired_sums(residual, precond, image)
    alpha = norm_now / product
    direction, along = (precond, image)
    for iteration in range(ITERS):
        solution = solution + alpha * direction
        residual = residual - alpha * along
        if iteration + 1 < ITERS:
            precond = residual / diagonal
            image = operate(precond, diagonal)
            norm_next, product = paired_sums(residual, precond, image)
            ratio = norm_next / norm_now
            alpha = norm_next / (product - ratio * norm_next / alpha)
            direction = precond + ratio * direction
            along = image + ratio * along
            norm_now = norm_next
    current = (base + slope * solution).reshape(-1)
    peers = link_count.shape[2]
    capacity = link_voxel.shape[2] // peers
    picked = current[link_voxel[0, 0]].reshape(peers, capacity)
    within = jnp.arange(capacity)
    live = within[None, :] < link_count[0, 0][:, None]
    outgoing = jnp.where(live, 0.5 * picked, jnp.float32(0.0))
    incoming = lax.all_to_all(outgoing, "gy", split_axis=0, concat_axis=0, tiled=True)
    totals = jax.ops.segment_sum(incoming.reshape(-1), link_target[0, 0], num_segments=PART_DEV)
    return (solution, totals.reshape(1, 1, PART_DEV))


def solution(mesh):
    return jax.shard_map(
        shards,
        mesh=mesh,
        in_specs=(
            P("gx", "gy", None),
            P("gx", "gy", None),
            P("gx", "gy", None),
            P("gx", "gy", None),
            P("gx", "gy", None),
            P("gx", "gy", None),
        ),
        out_specs=(P("gx", "gy", None), P("gx", "gy", None)),
        check_vma=False,
    )
```

profile of v0, /device:TPU:0, one launch (start us, length us, event | category | flops | bytes accessed | tf_op | source)
XLA Modules:
  0.0 851.8 jit_solution(11301537836566449882)
XLA Ops:
  4.4 5.6 collective-permute-start.1
  13.4 3.0 collective-permute-start.3
  20.7 44.0 %all-reduce.23 = (f32[]{:T(128)}, f32[]{:T(128)}) all-reduce(f32[]{:T(128)} %get-tuple-element.25, f32[]{:T(128)} %get-tuple-element.24), channel_id=1, replica_groups=mesh['gx'=4,'gy'=8] {'gx','gy'}, use_global_device_ids=true, to_apply=%region_1.2 | all-reduce | flops 2 | bytes 16 | tf_op jit(solution)/shard_map/psum | solution.py:45
  69.2 4.5 collective-permute-start.5
  77.0 3.0 collective-permute-start.7
  84.4 44.4 %all-reduce.22 = (f32[]{:T(128)}, f32[]{:T(128)}) all-reduce(f32[]{:T(128)} %get-tuple-element.23, f32[]{:T(128)} %get-tuple-element.22), channel_id=1, replica_groups=mesh['gx'=4,'gy'=8] {'gx','gy'}, use_global_device_ids=true, to_apply=%region_5.6 | all-reduce | flops 2 | bytes 16 | tf_op jit(solution)/shard_map/psum | solution.py:45
  137.1 4.5 collective-permute-start.9
  144.9 3.0 collective-permute-start.11
  152.2 44.3 %all-reduce.21 = (f32[]{:T(128)}, f32[]{:T(128)}) all-reduce(f32[]{:T(128)} %get-tuple-element.21, f32[]{:T(128)} %get-tuple-element.20), channel_id=1, replica_groups=mesh['gx'=4,'gy'=8] {'gx','gy'}, use_global_device_ids=true, to_apply=%region_9.10 | all-reduce | flops 2 | bytes 16 | tf_op jit(solution)/shard_map/psum | solution.py:45
  200.7 3.8 fusion.69
  205.8 4.5 collective-permute-start.13
  213.7 3.5 collective-permute-start.15
  221.0 44.3 %all-reduce.20 = (f32[]{:T(128)}, f32[]{:T(128)}) all-reduce(f32[]{:T(128)} %get-tuple-element.19, f32[]{:T(128)} %get-tuple-element.18), channel_id=1, replica_groups=mesh['gx'=4,'gy'=8] {'gx','gy'}, use_global_device_ids=true, to_apply=%region_13.14 | all-reduce | flops 2 | bytes 16 | tf_op jit(solution)/shard_map/psum | solution.py:45
  273.1 4.5 collective-permute-start.17
  280.9 3.0 collective-permute-start.19
  285.7 2.6 multiply_reduce_fusion.13
  288.3 44.3 %all-reduce.19 = (f32[]{:T(128)}, f32[]{:T(128)}) all-reduce(f32[]{:T(128)} %get-tuple-element.17, f32[]{:T(128)} %get-tuple-element.16), channel_id=1, replica_groups=mesh['gx'=4,'gy'=8] {'gx','gy'}, use_global_device_ids=true, to_apply=%region_17.18 | all-reduce | flops 2 | bytes 16 | tf_op jit(solution)/shard_map/psum | solution.py:45
  336.4 3.8 fusion.65
  341.5 4.5 collective-permute-start.21
  349.3 3.0 collective-permute-start.23
  356.7 44.2 %all-reduce.18 = (f32[]{:T(128)}, f32[]{:T(128)}) all-reduce(f32[]{:T(128)} %get-tuple-element.15, f32[]{:T(128)} %get-tuple-element.14), channel_id=1, replica_groups=mesh['gx'=4,'gy'=8] {'gx','gy'}, use_global_device_ids=true, to_apply=%region_21.22 | all-reduce | flops 2 | bytes 16 | tf_op jit(solution)/shard_map/psum | solution.py:45
  408.2 4.5 collective-permute-start.25
  416.0 3.2 collective-permute-start.27
  420.7 2.6 multiply_reduce_fusion.9
  423.3 44.2 %all-reduce.17 = (f32[]{:T(128)}, f32[]{:T(128)}) all-reduce(f32[]{:T(128)} %get-tuple-element.13, f32[]{:T(128)} %get-tuple-element.12), channel_id=1, replica_groups=mesh['gx'=4,'gy'=8] {'gx','gy'}, use_global_device_ids=true, to_apply=%region_25.26 | all-reduce | flops 2 | bytes 16 | tf_op jit(solution)/shard_map/psum | solution.py:45
  471.4 3.8 fusion.61
  476.6 4.5 collective-permute-start.29
  484.4 3.0 collective-permute-start.31
  491.7 44.3 %all-reduce.16 = (f32[]{:T(128)}, f32[]{:T(128)}) all-reduce(f32[]{:T(128)} %get-tuple-element.11, f32[]{:T(128)} %get-tuple-element.10), channel_id=1, replica_groups=mesh['gx'=4,'gy'=8] {'gx','gy'}, use_global_device_ids=true, to_apply=%region_29.30 | all-reduce | flops 2 | bytes 16 | tf_op jit(solution)/shard_map/psum | solution.py:45
  543.7 4.5 collective-permute-start.33
  551.5 3.0 collective-permute-start.35
  558.8 44.3 %all-reduce.15 = (f32[]{:T(128)}, f32[]{:T(128)}) all-reduce(f32[]{:T(128)} %get-tuple-element.9, f32[]{:T(128)} %get-tuple-element.8), channel_id=1, replica_groups=mesh['gx'=4,'gy'=8] {'gx','gy'}, use_global_device_ids=true, to_apply=%region_33.34 | all-reduce | flops 2 | bytes 16 | tf_op jit(solution)/shard_map/psum | solution.py:45
  607.1 3.8 fusion.57
  612.2 4.5 collective-permute-start.37
  620.0 3.2 collective-permute-start.39
  627.4 44.3 %all-reduce.14 = (f32[]{:T(128)}, f32[]{:T(128)}) all-reduce(f32[]{:T(128)} %get-tuple-element.7, f32[]{:T(128)} %get-tuple-element.6), channel_id=1, replica_groups=mesh['gx'=4,'gy'=8] {'gx','gy'}, use_global_device_ids=true, to_apply=%region_37.38 | all-reduce | flops 2 | bytes 16 | tf_op jit(solution)/shard_map/psum | solution.py:45
  679.3 4.5 collective-permute-start.41
  687.1 3.0 collective-permute-start.43
  691.9 2.6 multiply_reduce_fusion.1
  694.5 44.2 %all-reduce.13 = (f32[]{:T(128)}, f32[]{:T(128)}) all-reduce(f32[]{:T(128)} %get-tuple-element.5, f32[]{:T(128)} %get-tuple-element.4), channel_id=1, replica_groups=mesh['gx'=4,'gy'=8] {'gx','gy'}, use_global_device_ids=true, to_apply=%region_41.42 | all-reduce | flops 2 | bytes 16 | tf_op jit(solution)/shard_map/psum | solution.py:45
  742.5 2.8 fusion.53
  746.7 4.5 collective-permute-start.45
  754.5 3.0 collective-permute-start.47
  760.8 44.2 %all-reduce.12 = (f32[]{:T(128)}, f32[]{:T(128)}) all-reduce(f32[]{:T(128)} %get-tuple-element.3, f32[]{:T(128)} %get-tuple-element.2), channel_id=1, replica_groups=mesh['gx'=4,'gy'=8] {'gx','gy'}, use_global_device_ids=true, to_apply=%region_45.46 | all-reduce | flops 2 | bytes 16 | tf_op jit(solution)/shard_map/psum | solution.py:45
  808.8 6.1 multiply_add_fusion
  815.2 11.8 %gather_fusion = f32[2048]{0:T(1024)S(1)} fusion(f32[262144]{0:T(1024)S(1)} %bitcast.10, s32[2048]{0:T(1024)S(1)} %broadcast_clamp_fusion), kind=kCustom, calls=%fused_computation | custom fusion | bytes 24576 | tf_op jit(solution)/shard_map/gather | solution.py:73
  827.1 9.2 %all_to_all.6 = f32[8,1,256]{2,1,0:T(1,128)S(1)} all-to-all(f32[8,1,256]{2,1,0:T(1,128)S(1)} %compare_select_fusion.1), channel_id=1, replica_groups=mesh['gx'=4,'gy'=8] {'gy'}, dimensions={0} | all-to-all | bytes 16384 | tf_op jit(solution)/shard_map/all_to_all | solution.py:77
  836.2 15.4 %scatter_custom_fusion = f32[512]{0:T(512)} fusion(s32[2048]{0:T(1024)} %bitcast.17, f32[2048]{0:T(1024)S(1)} %bitcast.14, f32[]{:T(128)} %constant.8.clone.1), kind=kCustom, calls=%fused_computation.312 | custom fusion | flops 2048 | bytes 2560 | tf_op jit(solution)/shard_map/scatter-add | solution.py:78
  (175 shorter events, 112.7 us)
Async XLA Ops:
  3.1 7.2 collective-permute-start
  4.4 7.5 collective-permute-start.1
  12.0 4.5 collective-permute-start.2
  13.4 3.9 collective-permute-start.3
  67.9 6.2 collective-permute-start.4
  69.2 6.4 collective-permute-start.5
  75.7 4.3 collective-permute-start.6
  77.0 3.9 collective-permute-start.7
  135.8 6.2 collective-permute-start.8
  137.1 6.4 collective-permute-start.9
  143.6 4.3 collective-permute-start.10
  144.9 3.9 collective-permute-start.11
  204.5 6.2 collective-permute-start.12
  205.8 6.4 collective-permute-start.13
  212.4 4.8 collective-permute-start.14
  213.7 3.9 collective-permute-start.15
  271.8 6.2 collective-permute-start.16
  273.1 6.4 collective-permute-start.17
  279.6 4.3 collective-permute-start.18
  280.9 3.9 collective-permute-start.19
  340.2 6.2 collective-permute-start.20
  341.5 6.4 collective-permute-start.21
  348.0 4.3 collective-permute-start.22
  349.3 3.9 collective-permute-start.23
  406.9 6.2 collective-permute-start.24
  408.2 6.4 collective-permute-start.25
  414.7 4.5 collective-permute-start.26
  416.0 3.9 collective-permute-start.27
  475.3 6.2 collective-permute-start.28
  476.6 6.4 collective-permute-start.29
  483.1 4.3 collective-permute-start.30
  484.4 3.9 collective-permute-start.31
  542.4 6.2 collective-permute-start.32
  543.7 6.4 collective-permute-start.33
  550.2 4.3 collective-permute-start.34
  551.5 3.9 collective-permute-start.35
  610.9 6.2 collective-permute-start.36
  612.2 6.4 collective-permute-start.37
  618.7 4.6 collective-permute-start.38
  620.0 3.9 collective-permute-start.39
  678.0 6.2 collective-permute-start.40
  679.3 6.4 collective-permute-start.41
  685.8 4.3 collective-permute-start.42
  687.1 3.9 collective-permute-start.43
  745.4 6.2 collective-permute-start.44
  746.7 6.4 collective-permute-start.45
  753.2 4.4 collective-permute-start.46
  754.5 3.9 collective-permute-start.47
  (23 other events, 304.2 us)
where the time goes:
time: 864 us; the launch traced here: 852 us
  blocking collectives  540 us (62%)
  starting transfers between devices  124 us (14%)
  other arithmetic  96.8 us (11%)
  between operations  47 us (5%)
  waiting for transfers between devices  31.8 us (4%)
  local copies, waits for them, and re-layouts  12.3 us (1%)
    psum x12, blocking collectives, paired_sums(): lax.psum((jnp.sum(residual * precond), jnp.sum(precond * image)), ('gx',...  531 us
    ppermute x24, starting transfers between devices, extended(): lax.ppermute(lax.slice_in_dim(block, block.shape[dim] - width, None, axis...  92.9 us
    div x12, other arithmetic, shards(): precond = residual / diagonal  34.3 us
    ppermute x24, starting transfers between devices, extended(): lax.ppermute(lax.slice_in_dim(block, 0, width, axis=dim), axis, backward)  31.1 us
    reduce_sum x12, other arithmetic, paired_sums(): jnp.sum(precond * image)  30 us
    ppermute x24, waiting for transfers between devices, extended(): lax.ppermute(lax.slice_in_dim(block, block.shape[dim] - width, None, axis...  28.1 us
  transfers between devices with their start and end apart: 48, of which 36 were waited for; matrix products, arithmetic and copies ran while one was open for 0% of the time, Pallas kernels for 0%

commit v1 on v0

--- a/solution.py
+++ b/solution.py
@@ -42,7 +42,7 @@
 
 
 def paired_sums(residual, precond, image):
-    return lax.psum((jnp.sum(residual * precond), jnp.sum(precond * image)), ("gx", "gy"))
+    return lax.psum(lax.psum((jnp.sum(residual * precond), jnp.sum(precond * image)), "gx"), "gy")
 
 
 def shards(source, voxel_phase, lin_potential, link_voxel, link_count, link_target):

time: 864 us -> 653 us (0.76)
  blocking collectives: 540 us -> 331 us
    psum x12 -> x24, blocking collectives: 531 us -> 322 us  [the longest x12 183 us: paired_sums(): lax.psum(lax.psum((jnp.sum(residual * precond), jnp.sum(precond * image))...]
where the time goes in v1:
time: 653 us; the launch traced here: 642 us
  blocking collectives  331 us (51%)
  starting transfers between devices  123 us (19%)
  other arithmetic  96.6 us (15%)
  between operations  45.8 us (7%)
  waiting for transfers between devices  32.4 us (5%)
  local copies, waits for them, and re-layouts  12.3 us (2%)
    psum x12, blocking collectives, paired_sums(): lax.psum(lax.psum((jnp.sum(residual * precond), jnp.sum(precond * image))...  183 us
    psum x12, blocking collectives, paired_sums(): lax.psum((jnp.sum(residual * precond), jnp.sum(precond * image)), 'gx')  139 us
    ppermute x24, starting transfers between devices, extended(): lax.ppermute(lax.slice_in_dim(block, block.shape[dim] - width, None, axis...  92.2 us
    div x12, other arithmetic, shards(): precond = residual / diagonal  34.3 us
    ppermute x24, starting transfers between devices, extended(): lax.ppermute(lax.slice_in_dim(block, 0, width, axis=dim), axis, backward)  31.1 us
    reduce_sum x12, other arithmetic, paired_sums(): jnp.sum(precond * image)  29.8 us
    ppermute x24, waiting for transfers between devices, extended(): lax.ppermute(lax.slice_in_dim(block, block.shape[dim] - width, None, axis...  27.9 us
    scatter-add x1, other arithmetic, shards(): jax.ops.segment_sum(incoming.reshape(-1), link_target[0, 0], num_segments...  15.4 us
  transfers between devices with their start and end apart: 48, of which 36 were waited for; matrix products, arithmetic and copies ran while one was open for 0% of the time, Pallas kernels for 0%

profile of v1, /device:TPU:0, one launch (start us, length us, event | category | flops | bytes accessed | tf_op | source)
XLA Modules:
  0.0 641.9 jit_solution(9252570461483400253)
XLA Ops:
  4.4 5.6 collective-permute-start.1
  20.7 13.9 %all-reduce.35 = (f32[]{:T(128)}, f32[]{:T(128)}) all-reduce(f32[]{:T(128)} %get-tuple-element.25, f32[]{:T(128)} %get-tuple-element.24), channel_id=1, replica_groups=mesh['gx'=4,'gy'=8] {'gx'}, use_global_device_ids=true, to_apply=%region_1.2 | all-reduce | flops 2 | bytes 16 | tf_op jit(solution)/shard_map/psum | solution.py:45
  34.5 13.9 %all-reduce.23 = (f32[]{:T(128)}, f32[]{:T(128)}) all-reduce(f32[]{:T(128)} %get-tuple-element.72, f32[]{:T(128)} %get-tuple-element.73), channel_id=1, replica_groups=mesh['gx'=4,'gy'=8] {'gy'}, use_global_device_ids=true, to_apply=%region_2.3 | all-reduce | flops 2 | bytes 16 | tf_op jit(solution)/shard_map/psum | solution.py:45
  53.0 4.5 collective-permute-start.5
  60.8 3.0 collective-permute-start.7
  68.2 11.4 %all-reduce.34 = (f32[]{:T(128)}, f32[]{:T(128)}) all-reduce(f32[]{:T(128)} %get-tuple-element.23, f32[]{:T(128)} %get-tuple-element.22), channel_id=1, replica_groups=mesh['gx'=4,'gy'=8] {'gx'}, use_global_device_ids=true, to_apply=%region_7.8 | all-reduce | flops 2 | bytes 16 | tf_op jit(solution)/shard_map/psum | solution.py:45
  79.5 14.3 %all-reduce.22 = (f32[]{:T(128)}, f32[]{:T(128)}) all-reduce(f32[]{:T(128)} %get-tuple-element.70, f32[]{:T(128)} %get-tuple-element.71), channel_id=1, replica_groups=mesh['gx'=4,'gy'=8] {'gy'}, use_global_device_ids=true, to_apply=%region_8.9 | all-reduce | flops 2 | bytes 16 | tf_op jit(solution)/shard_map/psum | solution.py:45
  101.9 4.5 collective-permute-start.9
  109.7 3.0 collective-permute-start.11
  117.1 11.4 %all-reduce.33 = (f32[]{:T(128)}, f32[]{:T(128)}) all-reduce(f32[]{:T(128)} %get-tuple-element.21, f32[]{:T(128)} %get-tuple-element.20), channel_id=1, replica_groups=mesh['gx'=4,'gy'=8] {'gx'}, use_global_device_ids=true, to_apply=%region_13.14 | all-reduce | flops 2 | bytes 16 | tf_op jit(solution)/shard_map/psum | solution.py:45
  128.5 15.4 %all-reduce.21 = (f32[]{:T(128)}, f32[]{:T(128)}) all-reduce(f32[]{:T(128)} %get-tuple-element.68, f32[]{:T(128)} %get-tuple-element.69), channel_id=1, replica_groups=mesh['gx'=4,'gy'=8] {'gy'}, use_global_device_ids=true, to_apply=%region_14.15 | all-reduce | flops 2 | bytes 16 | tf_op jit(solution)/shard_map/psum | solution.py:45
  147.6 3.8 fusion.69
  152.8 4.5 collective-permute-start.13
  160.6 3.0 collective-permute-start.15
  167.9 11.4 %all-reduce.32 = (f32[]{:T(128)}, f32[]{:T(128)}) all-reduce(f32[]{:T(128)} %get-tuple-element.19, f32[]{:T(128)} %get-tuple-element.18), channel_id=1, replica_groups=mesh['gx'=4,'gy'=8] {'gx'}, use_global_device_ids=true, to_apply=%region_19.20 | all-reduce | flops 2 | bytes 16 | tf_op jit(solution)/shard_map/psum | solution.py:45
  179.3 15.8 %all-reduce.20 = (f32[]{:T(128)}, f32[]{:T(128)}) all-reduce(f32[]{:T(128)} %get-tuple-element.66, f32[]{:T(128)} %get-tuple-element.67), channel_id=1, replica_groups=mesh['gx'=4,'gy'=8] {'gy'}, use_global_device_ids=true, to_apply=%region_20.21 | all-reduce | flops 2 | bytes 16 | tf_op jit(solution)/shard_map/psum | solution.py:45
  202.7 4.5 collective-permute-start.17
  217.8 11.4 %all-reduce.31 = (f32[]{:T(128)}, f32[]{:T(128)}) all-reduce(f32[]{:T(128)} %get-tuple-element.17, f32[]{:T(128)} %get-tuple-element.16), channel_id=1, replica_groups=mesh['gx'=4,'gy'=8] {'gx'}, use_global_device_ids=true, to_apply=%region_25.26 | all-reduce | flops 2 | bytes 16 | tf_op jit(solution)/shard_map/psum | solution.py:45
  229.2 15.3 %all-reduce.19 = (f32[]{:T(128)}, f32[]{:T(128)}) all-reduce(f32[]{:T(128)} %get-tuple-element.64, f32[]{:T(128)} %get-tuple-element.65), channel_id=1, replica_groups=mesh['gx'=4,'gy'=8] {'gy'}, use_global_device_ids=true, to_apply=%region_26.27 | all-reduce | flops 2 | bytes 16 | tf_op jit(solution)/shard_map/psum | solution.py:45
  248.3 3.8 fusion.65
  253.4 4.5 collective-permute-start.21
  268.6 11.4 %all-reduce.30 = (f32[]{:T(128)}, f32[]{:T(128)}) all-reduce(f32[]{:T(128)} %get-tuple-element.15, f32[]{:T(128)} %get-tuple-element.14), channel_id=1, replica_groups=mesh['gx'=4,'gy'=8] {'gx'}, use_global_device_ids=true, to_apply=%region_31.32 | all-reduce | flops 2 | bytes 16 | tf_op jit(solution)/shard_map/psum | solution.py:45
  280.0 15.4 %all-reduce.18 = (f32[]{:T(128)}, f32[]{:T(128)}) all-reduce(f32[]{:T(128)} %get-tuple-element.62, f32[]{:T(128)} %get-tuple-element.63), channel_id=1, replica_groups=mesh['gx'=4,'gy'=8] {'gy'}, use_global_device_ids=true, to_apply=%region_32.33 | all-reduce | flops 2 | bytes 16 | tf_op jit(solution)/shard_map/psum | solution.py:45
  302.8 4.5 collective-permute-start.25
  317.9 11.3 %all-reduce.29 = (f32[]{:T(128)}, f32[]{:T(128)}) all-reduce(f32[]{:T(128)} %get-tuple-element.13, f32[]{:T(128)} %get-tuple-element.12), channel_id=1, replica_groups=mesh['gx'=4,'gy'=8] {'gx'}, use_global_device_ids=true, to_apply=%region_37.38 | all-reduce | flops 2 | bytes 16 | tf_op jit(solution)/shard_map/psum | solution.py:45
  329.2 15.3 %all-reduce.17 = (f32[]{:T(128)}, f32[]{:T(128)}) all-reduce(f32[]{:T(128)} %get-tuple-element.60, f32[]{:T(128)} %get-tuple-element.61), channel_id=1, replica_groups=mesh['gx'=4,'gy'=8] {'gy'}, use_global_device_ids=true, to_apply=%region_38.39 | all-reduce | flops 2 | bytes 16 | tf_op jit(solution)/shard_map/psum | solution.py:45
  348.3 3.8 fusion.61
  353.4 4.5 collective-permute-start.29
  368.5 11.3 %all-reduce.28 = (f32[]{:T(128)}, f32[]{:T(128)}) all-reduce(f32[]{:T(128)} %get-tuple-element.11, f32[]{:T(128)} %get-tuple-element.10), channel_id=1, replica_groups=mesh['gx'=4,'gy'=8] {'gx'}, use_global_device_ids=true, to_apply=%region_43.44 | all-reduce | flops 2 | bytes 16 | tf_op jit(solution)/shard_map/psum | solution.py:45
  379.8 15.5 %all-reduce.16 = (f32[]{:T(128)}, f32[]{:T(128)}) all-reduce(f32[]{:T(128)} %get-tuple-element.58, f32[]{:T(128)} %get-tuple-element.59), channel_id=1, replica_groups=mesh['gx'=4,'gy'=8] {'gy'}, use_global_device_ids=true, to_apply=%region_44.45 | all-reduce | flops 2 | bytes 16 | tf_op jit(solution)/shard_map/psum | solution.py:45
  402.6 4.5 collective-permute-start.33
  417.7 11.4 %all-reduce.27 = (f32[]{:T(128)}, f32[]{:T(128)}) all-reduce(f32[]{:T(128)} %get-tuple-element.9, f32[]{:T(128)} %get-tuple-element.8), channel_id=1, replica_groups=mesh['gx'=4,'gy'=8] {'gx'}, use_global_device_ids=true, to_apply=%region_49.50 | all-reduce | flops 2 | bytes 16 | tf_op jit(solution)/shard_map/psum | solution.py:45
  429.1 15.4 %all-reduce.15 = (f32[]{:T(128)}, f32[]{:T(128)}) all-reduce(f32[]{:T(128)} %get-tuple-element.56, f32[]{:T(128)} %get-tuple-element.57), channel_id=1, replica_groups=mesh['gx'=4,'gy'=8] {'gy'}, use_global_device_ids=true, to_apply=%region_50.51 | all-reduce | flops 2 | bytes 16 | tf_op jit(solution)/shard_map/psum | solution.py:45
  448.3 3.8 fusion.57
  453.5 4.5 collective-permute-start.37
  468.6 11.4 %all-reduce.26 = (f32[]{:T(128)}, f32[]{:T(128)}) all-reduce(f32[]{:T(128)} %get-tuple-element.7, f32[]{:T(128)} %get-tuple-element.6), channel_id=1, replica_groups=mesh['gx'=4,'gy'=8] {'gx'}, use_global_device_ids=true, to_apply=%region_55.56 | all-reduce | flops 2 | bytes 16 | tf_op jit(solution)/shard_map/psum | solution.py:45
  480.0 15.4 %all-reduce.14 = (f32[]{:T(128)}, f32[]{:T(128)}) all-reduce(f32[]{:T(128)} %get-tuple-element.54, f32[]{:T(128)} %get-tuple-element.55), channel_id=1, replica_groups=mesh['gx'=4,'gy'=8] {'gy'}, use_global_device_ids=true, to_apply=%region_56.57 | all-reduce | flops 2 | bytes 16 | tf_op jit(solution)/shard_map/psum | solution.py:45
  502.9 4.5 collective-permute-start.41
  518.1 11.4 %all-reduce.25 = (f32[]{:T(128)}, f32[]{:T(128)}) all-reduce(f32[]{:T(128)} %get-tuple-element.5, f32[]{:T(128)} %get-tuple-element.4), channel_id=1, replica_groups=mesh['gx'=4,'gy'=8] {'gx'}, use_global_device_ids=true, to_apply=%region_61.62 | all-reduce | flops 2 | bytes 16 | tf_op jit(solution)/shard_map/psum | solution.py:45
  529.5 15.4 %all-reduce.13 = (f32[]{:T(128)}, f32[]{:T(128)}) all-reduce(f32[]{:T(128)} %get-tuple-element.52, f32[]{:T(128)} %get-tuple-element.53), channel_id=1, replica_groups=mesh['gx'=4,'gy'=8] {'gy'}, use_global_device_ids=true, to_apply=%region_62.63 | all-reduce | flops 2 | bytes 16 | tf_op jit(solution)/shard_map/psum | solution.py:45
  553.0 4.5 collective-permute-start.45
  560.8 3.2 collective-permute-start.47
  567.2 11.4 %all-reduce.24 = (f32[]{:T(128)}, f32[]{:T(128)}) all-reduce(f32[]{:T(128)} %get-tuple-element.3, f32[]{:T(128)} %get-tuple-element.2), channel_id=1, replica_groups=mesh['gx'=4,'gy'=8] {'gx'}, use_global_device_ids=true, to_apply=%region_67.68 | all-reduce | flops 2 | bytes 16 | tf_op jit(solution)/shard_map/psum | solution.py:45
  578.6 15.4 %all-reduce.12 = (f32[]{:T(128)}, f32[]{:T(128)}) all-reduce(f32[]{:T(128)} %get-tuple-element.50, f32[]{:T(128)} %get-tuple-element.51), channel_id=1, replica_groups=mesh['gx'=4,'gy'=8] {'gy'}, use_global_device_ids=true, to_apply=%region_68.69 | all-reduce | flops 2 | bytes 16 | tf_op jit(solution)/shard_map/psum | solution.py:45
  598.1 6.1 multiply_add_fusion
  604.5 11.8 %gather_fusion = f32[2048]{0:T(1024)S(1)} fusion(f32[262144]{0:T(1024)S(1)} %bitcast.10, s32[2048]{0:T(1024)S(1)} %broadcast_clamp_fusion), kind=kCustom, calls=%fused_computation | custom fusion | bytes 24576 | tf_op jit(solution)/shard_map/gather | solution.py:73
  616.4 9.9 %all_to_all.6 = f32[8,1,256]{2,1,0:T(1,128)S(1)} all-to-all(f32[8,1,256]{2,1,0:T(1,128)S(1)} %compare_select_fusion.1), channel_id=1, replica_groups=mesh['gx'=4,'gy'=8] {'gy'}, dimensions={0} | all-to-all | bytes 16384 | tf_op jit(solution)/shard_map/all_to_all | solution.py:77
  626.3 15.4 %scatter_custom_fusion = f32[512]{0:T(512)} fusion(s32[2048]{0:T(1024)} %bitcast.17, f32[2048]{0:T(1024)S(1)} %bitcast.14, f32[]{:T(128)} %constant.8.clone.1), kind=kCustom, calls=%fused_computation.312 | custom fusion | flops 2048 | bytes 2560 | tf_op jit(solution)/shard_map/scatter-add | solution.py:78
  (187 shorter events, 148.1 us)
Async XLA Ops:
  3.1 7.2 %collective-permute-start = (f32[1,32,512]{2,1,0:T(8,128)S(1)}, f32[1,32,512]{2,1,0:T(8,128)S(1)}, u32[]{:S(2)}, u32[]{:S(2)}) collective-permute-start(f32[1,32,512]{2,1,0:T(8,128)S(1)} %get-tuple-element.162), channel_id=1, source_target_pairs={{8,0},{16,8},{24,16},{9,1},{17,9},{25,17},{10,2},{18,10},{26,18},{... | collective-permute-start | bytes 196616 | tf_op jit(solution)/shard_map/ppermute | solution.py:18
  4.4 7.5 %collective-permute-start.1 = (f32[1,32,512]{2,1,0:T(8,128)S(1)}, f32[1,32,512]{2,1,0:T(8,128)S(1)}, u32[]{:S(2)}, u32[]{:S(2)}) collective-permute-start(f32[1,32,512]{2,1,0:T(8,128)S(1)} %get-tuple-element.161), channel_id=1, source_target_pairs={{0,8},{8,16},{16,24},{1,9},{9,17},{17,25},{2,10},{10,18},{18,26},{... | collective-permute-start | bytes 196616 | tf_op jit(solution)/shard_map/ppermute | solution.py:15
  12.0 4.5 collective-permute-start.2
  13.4 3.9 collective-permute-start.3
  51.7 6.2 collective-permute-start.4
  53.0 6.4 %collective-permute-start.5 = (f32[1,32,512]{2,1,0:T(8,128)S(1)}, f32[1,32,512]{2,1,0:T(8,128)S(1)}, u32[]{:S(2)}, u32[]{:S(2)}) collective-permute-start(f32[1,32,512]{2,1,0:T(8,128)S(1)} %get-tuple-element.159), channel_id=1, source_target_pairs={{0,8},{8,16},{16,24},{1,9},{9,17},{17,25},{2,10},{10,18},{18,26},{... | collective-permute-start | bytes 196616 | tf_op jit(solution)/shard_map/ppermute | solution.py:15
  59.5 4.3 collective-permute-start.6
  60.8 3.9 collective-permute-start.7
  100.6 6.2 collective-permute-start.8
  101.9 6.4 %collective-permute-start.9 = (f32[1,32,512]{2,1,0:T(8,128)S(1)}, f32[1,32,512]{2,1,0:T(8,128)S(1)}, u32[]{:S(2)}, u32[]{:S(2)}) collective-permute-start(f32[1,32,512]{2,1,0:T(8,128)S(1)} %get-tuple-element.157), channel_id=1, source_target_pairs={{0,8},{8,16},{16,24},{1,9},{9,17},{17,25},{2,10},{10,18},{18,26},{... | collective-permute-start | bytes 196616 | tf_op jit(solution)/shard_map/ppermute | solution.py:15
  108.4 4.3 collective-permute-start.10
  109.7 3.9 collective-permute-start.11
  151.5 6.2 collective-permute-start.12
  152.8 6.4 %collective-permute-start.13 = (f32[1,32,512]{2,1,0:T(8,128)S(1)}, f32[1,32,512]{2,1,0:T(8,128)S(1)}, u32[]{:S(2)}, u32[]{:S(2)}) collective-permute-start(f32[1,32,512]{2,1,0:T(8,128)S(1)} %get-tuple-element.155), channel_id=1, source_target_pairs={{0,8},{8,16},{16,24},{1,9},{9,17},{17,25},{2,10},{10,18},{18,26},{... | collective-permute-start | bytes 196616 | tf_op jit(solution)/shard_map/ppermute | solution.py:15
  159.3 4.3 collective-permute-start.14
  160.6 3.9 collective-permute-start.15
  201.4 6.2 collective-permute-start.16
  202.7 6.4 %collective-permute-start.17 = (f32[1,32,512]{2,1,0:T(8,128)S(1)}, f32[1,32,512]{2,1,0:T(8,128)S(1)}, u32[]{:S(2)}, u32[]{:S(2)}) collective-permute-start(f32[1,32,512]{2,1,0:T(8,128)S(1)} %get-tuple-element.153), channel_id=1, source_target_pairs={{0,8},{8,16},{16,24},{1,9},{9,17},{17,25},{2,10},{10,18},{18,26},{... | collective-permute-start | bytes 196616 | tf_op jit(solution)/shard_map/ppermute | solution.py:15
  209.2 4.3 collective-permute-start.18
  210.5 3.9 collective-permute-start.19
  252.1 6.2 collective-permute-start.20
  253.4 6.4 %collective-permute-start.21 = (f32[1,32,512]{2,1,0:T(8,128)S(1)}, f32[1,32,512]{2,1,0:T(8,128)S(1)}, u32[]{:S(2)}, u32[]{:S(2)}) collective-permute-start(f32[1,32,512]{2,1,0:T(8,128)S(1)} %get-tuple-element.151), channel_id=1, source_target_pairs={{0,8},{8,16},{16,24},{1,9},{9,17},{17,25},{2,10},{10,18},{18,26},{... | collective-permute-start | bytes 196616 | tf_op jit(solution)/shard_map/ppermute | solution.py:15
  259.9 4.3 collective-permute-start.22
  261.2 3.9 collective-permute-start.23
  301.5 6.2 collective-permute-start.24
  302.8 6.4 %collective-permute-start.25 = (f32[1,32,512]{2,1,0:T(8,128)S(1)}, f32[1,32,512]{2,1,0:T(8,128)S(1)}, u32[]{:S(2)}, u32[]{:S(2)}) collective-permute-start(f32[1,32,512]{2,1,0:T(8,128)S(1)} %get-tuple-element.149), channel_id=1, source_target_pairs={{0,8},{8,16},{16,24},{1,9},{9,17},{17,25},{2,10},{10,18},{18,26},{... | collective-permute-start | bytes 196616 | tf_op jit(solution)/shard_map/ppermute | solution.py:15
  309.3 4.3 collective-permute-start.26
  310.6 3.9 collective-permute-start.27
  352.1 6.2 collective-permute-start.28
  353.4 6.4 %collective-permute-start.29 = (f32[1,32,512]{2,1,0:T(8,128)S(1)}, f32[1,32,512]{2,1,0:T(8,128)S(1)}, u32[]{:S(2)}, u32[]{:S(2)}) collective-permute-start(f32[1,32,512]{2,1,0:T(8,128)S(1)} %get-tuple-element.147), channel_id=1, source_target_pairs={{0,8},{8,16},{16,24},{1,9},{9,17},{17,25},{2,10},{10,18},{18,26},{... | collective-permute-start | bytes 196616 | tf_op jit(solution)/shard_map/ppermute | solution.py:15
  359.9 4.3 collective-permute-start.30
  361.2 3.9 collective-permute-start.31
  401.3 6.2 collective-permute-start.32
  402.6 6.4 %collective-permute-start.33 = (f32[1,32,512]{2,1,0:T(8,128)S(1)}, f32[1,32,512]{2,1,0:T(8,128)S(1)}, u32[]{:S(2)}, u32[]{:S(2)}) collective-permute-start(f32[1,32,512]{2,1,0:T(8,128)S(1)} %get-tuple-element.145), channel_id=1, source_target_pairs={{0,8},{8,16},{16,24},{1,9},{9,17},{17,25},{2,10},{10,18},{18,26},{... | collective-permute-start | bytes 196616 | tf_op jit(solution)/shard_map/ppermute | solution.py:15
  409.1 4.3 collective-permute-start.34
  410.4 3.9 collective-permute-start.35
  452.2 6.2 collective-permute-start.36
  453.5 6.4 %collective-permute-start.37 = (f32[1,32,512]{2,1,0:T(8,128)S(1)}, f32[1,32,512]{2,1,0:T(8,128)S(1)}, u32[]{:S(2)}, u32[]{:S(2)}) collective-permute-start(f32[1,32,512]{2,1,0:T(8,128)S(1)} %get-tuple-element.143), channel_id=1, source_target_pairs={{0,8},{8,16},{16,24},{1,9},{9,17},{17,25},{2,10},{10,18},{18,26},{... | collective-permute-start | bytes 196616 | tf_op jit(solution)/shard_map/ppermute | solution.py:15
  460.0 4.3 collective-permute-start.38
  461.3 3.9 collective-permute-start.39
  501.6 6.2 collective-permute-start.40
  502.9 6.4 %collective-permute-start.41 = (f32[1,32,512]{2,1,0:T(8,128)S(1)}, f32[1,32,512]{2,1,0:T(8,128)S(1)}, u32[]{:S(2)}, u32[]{:S(2)}) collective-permute-start(f32[1,32,512]{2,1,0:T(8,128)S(1)} %get-tuple-element.141), channel_id=1, source_target_pairs={{0,8},{8,16},{16,24},{1,9},{9,17},{17,25},{2,10},{10,18},{18,26},{... | collective-permute-start | bytes 196616 | tf_op jit(solution)/shard_map/ppermute | solution.py:15
  509.4 4.3 collective-permute-start.42
  510.7 3.9 collective-permute-start.43
  551.7 6.2 collective-permute-start.44
  553.0 6.4 %collective-permute-start.45 = (f32[1,32,512]{2,1,0:T(8,128)S(1)}, f32[1,32,512]{2,1,0:T(8,128)S(1)}, u32[]{:S(2)}, u32[]{:S(2)}) collective-permute-start(f32[1,32,512]{2,1,0:T(8,128)S(1)} %get-tuple-element.139), channel_id=1, source_target_pairs={{0,8},{8,16},{16,24},{1,9},{9,17},{17,25},{2,10},{10,18},{18,26},{... | collective-permute-start | bytes 196616 | tf_op jit(solution)/shard_map/ppermute | solution.py:15
  559.5 4.6 collective-permute-start.46
  560.8 3.9 collective-permute-start.47
  (23 other events, 304.2 us)
